TPU v7x, 32 devices: a whole 2x2x4 slice. The times are simulated.
32 devices in a mesh: tile: 8 (over z, x), tp: 4 (over y, core).
Axes of the slice: x: 2, y: 2, z: 4, core: 2. Of those that a mesh axis runs over, the one named last changes fastest.
Arguments:
- latent: bfloat16 [512, 1024], P(('tile', 'tp')), may hold values from -6 to 6
- weight_in: bfloat16 [1024, 4096], P(None, 'tp'), may hold values from -0.1875 to 0.1875
- weight_out: bfloat16 [4096, 1024], P('tp'), may hold values from -0.09375 to 0.09375
- weight_conv: bfloat16 [7168, 2048], P(None, 'tp'), may hold values from -0.0625 to 0.0625
- neighbours: int32 [512, 7], P('tile'), may hold values from 0 to 96, as said below
- child_order: int32 [2048], P(('tile', 'tp')), may hold values from 0 to 63, as said below
- cotangent: bfloat16 [2048, 512], P(('tile', 'tp')), may hold values from -6 to 6
Outputs:
- fine_cells: bfloat16 [2048, 512], P(('tile', 'tp'))
- grad_latent: float32 [512, 1024], P(('tile', 'tp'))
- weight_in_grad: float32 [1024, 4096], P('tile', 'tp')
- weight_out_grad: float32 [4096, 1024], P('tp', 'tile')
- weight_conv_grad: float32 [7168, 2048], P('tile', 'tp')
Inputs may be any that keep to these rules, and one draw needn't show every extreme that they name: `neighbours`: column 0 of the row of a tile's i-th cell is i + 16 (the cell itself); the other columns lie within 16 of it, except that index 96, the empty row, marks a missing sixth neighbour of a pentagon cell. `child_order`: each block of 64 consecutive entries is a permutation of 0 .. 63.
All inputs are finite; a program needn't handle non-finite values.
Results may differ from a plain program's by a relative error of at most 0.02.
Values may be sent and summed in bfloat16 or wider, within the bound.
No kernel may reach another device: no remote copies, remote signals or barrier semaphores. Data moves between devices by JAX's collectives and lax.ppermute only.
A program may use at most 128 MiB of HBM per device.

v0:
```python
import math
import jax
import jax.numpy as jnp
from jax import lax
from jax.sharding import PartitionSpec as P

SLOTS = 4
HALO = 16
EPSILON = 1e-05


def with_halo(value, sides, width):
    for axis, dim in sides:
        count, length = (lax.axis_size(axis), value.shape[dim])
        up = [(i, (i + 1) % count) for i in range(count - 1)]
        down = [(j, i) for i, j in up]
        last = lax.slice_in_dim(value, length - width, length, axis=dim)
        initial = lax.slice_in_dim(value, 0, width, axis=dim)
        before = lax.ppermute(last, axis, up)
        after = lax.ppermute(initial, axis, down)
        value = jnp.concatenate([before, value, after], axis=dim)
    return value


def silu_grad(pre_value):
    sigmoid = jax.nn.sigmoid(pre_value)
    return sigmoid * (1.0 + pre_value * (1.0 - sigmoid))


def tp_rows(pieces):
    return lax.all_gather(pieces, "tp", axis=0, tiled=True)


def tp_sums(terms):
    return lax.psum(terms.astype(jnp.bfloat16), "tp").astype(jnp.float32)


def tile_margin(tile_data):
    return with_halo(tile_data, (("tile", 0),), HALO)


def regroup(block_data):
    return lax.all_to_all(block_data, "tp", split_axis=0, concat_axis=0, tiled=True)


def local(latent, weight_in, weight_out, weight_conv, neighbours, child_order, cotangent):
    groups = lax.axis_size("tp")
    tiles = lax.axis_size("tile")
    sub_rows = latent.shape[0]
    features = latent.shape[1]
    tile_rows = sub_rows * groups
    grad_scale = 1.0 / math.sqrt(tile_rows * tiles)
    tap_count = neighbours.shape[1]
    shard_cols = weight_conv.shape[1]
    shard_chans = shard_cols // SLOTS
    own_start = lax.axis_index("tp") * sub_rows
    source = latent.astype(jnp.float32)
    whole_source = tp_rows(latent).astype(jnp.float32)
    tile_norm = lax.rsqrt(jnp.mean(whole_source * whole_source, axis=1, keepdims=True) + EPSILON)
    norm_factor = lax.dynamic_slice_in_dim(tile_norm, own_start, sub_rows, 0)
    normed = (whole_source * tile_norm).astype(jnp.bfloat16)
    pre_act = jnp.dot(normed, weight_in, preferred_element_type=jnp.float32)
    hidden = jax.nn.silu(pre_act).astype(jnp.bfloat16)
    mixed = tp_sums(jnp.dot(hidden, weight_out, preferred_element_type=jnp.float32))
    latent_tile = (whole_source + mixed).astype(jnp.bfloat16)
    extended = jnp.concatenate(
        [tile_margin(latent_tile), jnp.zeros((1, features), jnp.bfloat16)], axis=0
    )
    tap_rows = jnp.take(extended, neighbours, axis=0).reshape(tile_rows, tap_count * features)
    coarse_out = jnp.dot(tap_rows, weight_conv, preferred_element_type=jnp.float32).astype(
        jnp.bfloat16
    )
    own_blocks = regroup(coarse_out)
    children = own_blocks.reshape(groups, sub_rows, shard_chans, SLOTS).transpose(1, 3, 0, 2)
    children = children.reshape(sub_rows * SLOTS, groups * shard_chans)
    activated = jax.nn.silu(children.astype(jnp.float32)).astype(jnp.bfloat16)
    fine_cells = jnp.take(activated, child_order, axis=0)
    child_grad = jnp.zeros_like(cotangent).at[child_order].set(cotangent)
    child_pre_grad = (
        child_grad.astype(jnp.float32) * silu_grad(children.astype(jnp.float32))
    ).astype(jnp.bfloat16)
    outgoing = child_pre_grad.reshape(sub_rows, SLOTS, groups, shard_chans).transpose(2, 0, 3, 1)
    coarse_grad = regroup(outgoing.reshape(groups * sub_rows, shard_cols))
    weight_conv_grad = lax.psum_scatter(
        (
            jnp.einsum("rk,rc->kc", tap_rows, coarse_grad, preferred_element_type=jnp.float32)
            * grad_scale
        ).astype(jnp.bfloat16),
        "tile",
        scatter_dimension=0,
        tiled=True,
    ).astype(jnp.float32)
    tap_grad = jnp.dot(coarse_grad, weight_conv.T, preferred_element_type=jnp.float32)
    tap_grad = tap_grad.reshape(tile_rows * tap_count, features)
    ext_grad = (
        jnp.zeros((tile_rows + 2 * HALO + 1, features), jnp.float32)
        .at[neighbours.reshape(-1)]
        .add(tap_grad)
    )
    rim_rows = jnp.concatenate(
        [ext_grad[:HALO], ext_grad[tile_rows + HALO : tile_rows + 2 * HALO]], axis=0
    ).astype(jnp.bfloat16)
    arrived = tile_margin(rim_rows).astype(jnp.float32)
    partial_value = ext_grad[HALO : HALO + tile_rows]
    partial_value = partial_value.at[:HALO].add(arrived[:HALO])
    partial_value = partial_value.at[tile_rows - HALO :].add(arrived[3 * HALO :])
    latent_grad = lax.psum_scatter(
        partial_value.astype(jnp.bfloat16), "tp", scatter_dimension=0, tiled=True
    ).astype(jnp.float32)
    upstream = tp_rows(latent_grad.astype(jnp.bfloat16))
    hidden_grad = jnp.dot(upstream, weight_out.T, preferred_element_type=jnp.float32)
    pre_grad = (hidden_grad * silu_grad(pre_act)).astype(jnp.bfloat16)
    out_term = (
        jnp.einsum("rf,rd->fd", hidden, upstream, preferred_element_type=jnp.float32) * grad_scale
    )
    weight_out_grad = lax.psum_scatter(
        out_term.astype(jnp.bfloat16), "tile", scatter_dimension=1, tiled=True
    ).astype(jnp.float32)
    normed_whole = tp_sums(jnp.dot(pre_grad, weight_in.T, preferred_element_type=jnp.float32))
    normed_grad = lax.dynamic_slice_in_dim(normed_whole, own_start, sub_rows, 0)
    grad_latent = (
        latent_grad
        + norm_factor * normed_grad
        - source
        * norm_factor
        * norm_factor
        * norm_factor
        * jnp.mean(normed_grad * source, axis=1, keepdims=True)
    )
    weight_in_grad = lax.psum_scatter(
        (
            jnp.einsum("rd,rf->df", normed, pre_grad, preferred_element_type=jnp.float32)
            * grad_scale
        ).astype(jnp.bfloat16),
        "tile",
        scatter_dimension=0,
        tiled=True,
    ).astype(jnp.float32)
    return (fine_cells, grad_latent, weight_in_grad, weight_out_grad, weight_conv_grad)


def solution(mesh):
    placed = (
        P(("tile", "tp"), None),
        P(None, "tp"),
        P("tp", None),
        P(None, "tp"),
        P("tile", None),
        P(("tile", "tp")),
        P(("tile", "tp"), None),
    )
    return jax.shard_map(
        local,
        mesh=mesh,
        in_specs=placed,
        out_specs=(
            P(("tile", "tp"), None),
            P(("tile", "tp"), None),
            P("tile", "tp"),
            P("tp", "tile"),
            P("tile", "tp"),
        ),
        check_vma=False,
    )
```

profile of v0, /device:TPU:0, one launch (start us, length us, event | category | flops | bytes accessed | tf_op | source)
XLA Modules:
  0.0 469.5 jit_solution(18033173362639526849)
XLA Ops:
  7.2 6.9 %all_gather.6 = bf16[64,1024]{1,0:T(8,128)(2,1)S(1)} all-gather(bf16[16,1024]{1,0:T(8,128)(2,1)} %param.11), channel_id=1, replica_groups=mesh['tile'=8,'tp'=4] {'tp'}, dimensions={0}, use_global_device_ids=true | all-gather | bytes 163840 | tf_op jit(solution)/shard_map/all_gather | solution.py:31
  17.8 33.3 %all-reduce.3.cloned.1.call-done = bf16[64,1024]{1,0:T(8,128)(2,1)} async-done(((bf16[64,1024]{1,0:T(8,128)(2,1)}), bf16[64,1024]{1,0:T(8,128)(2,1)}) %all-reduce.3.cloned.1.call-update) | async-done | bytes 131088 | tf_op jit(solution)/shard_map/psum | solution.py:35
  52.1 3.4 collective-permute-start
  57.0 4.2 collective-permute-done.1
  61.4 2.7 gather_fusion
  68.3 5.1 %convolution_convert_fusion.2 = bf16[64,512]{1,0:T(8,128)(2,1)} fusion(bf16[64,7168]{1,0:T(8,128)(2,1)S(1)} %bitcast.55, bf16[7168,512]{1,0:T(8,128)(2,1)} %param.14), kind=kOutput, calls=%fused_computation.11 | convolution fusion | flops 469794816 | bytes 8323072 | tf_op jit(solution)/shard_map/dot_general | solution.py:70
  73.4 3.3 all-to-all-start
  78.1 2.7 all-to-all-done
  86.6 3.3 all-to-all-start.1
  89.9 4.0 all-to-all-done.1
  93.9 6.6 %fusion.29 = f32[64,7168]{1,0:T(8,128)} fusion(bf16[64,512]{1,0:T(8,128)(2,1)S(1)} %bitcast.61, bf16[7168,512]{1,0:T(8,128)(2,1)} %param.14), kind=kOutput, calls=%fused_computation.66 | convolution fusion | flops 469762048 | bytes 9240576 | tf_op jit(solution)/shard_map/dot_general | solution.py:93
  100.6 2.7 reshape.194
  103.3 5.8 %scatter_custom_fusion.1 = f32[97,1024]{1,0:T(8,128)} fusion(s32[448]{0:T(512)S(1)} %bitcast.65, f32[448,1024]{1,0:T(8,128)} %reshape.194, f32[]{:T(128)} %constant.110.clone.1), kind=kCustom, calls=%fused_computation.22 | custom fusion | flops 458752 | bytes 397824 | tf_op jit(solution)/shard_map/scatter-add | solution.py:98
  110.1 4.3 collective-permute-start.2
  116.7 3.5 collective-permute-done.3
  121.8 18.8 %reduce-scatter.7.cloned.1.call-done = bf16[16,1024]{1,0:T(8,128)(2,1)} async-done(((bf16[64,1024]{1,0:T(8,128)(2,1)}), bf16[16,1024]{1,0:T(8,128)(2,1)}) %reduce-scatter.7.cloned.1.call-update) | async-done | bytes 32784 | tf_op jit(solution)/shard_map/reduce_scatter | solution.py:107
  140.7 5.9 %all_gather.7 = bf16[64,1024]{1,0:T(8,128)(2,1)S(1)} all-gather(bf16[16,1024]{1,0:T(8,128)(2,1)} %reduce-scatter.7.cloned.1.call-done), channel_id=1, replica_groups=mesh['tile'=8,'tp'=4] {'tp'}, dimensions={0}, use_global_device_ids=true | all-gather | bytes 163840 | tf_op jit(solution)/shard_map/all_gather | solution.py:31
  149.8 3.1 multiply_convert_fusion.1
  152.9 4.0 copy.34
  159.1 5.1 %multiply_convert_fusion = bf16[7168,512]{1,0:T(8,128)(2,1)} fusion(bf16[64,7168]{1,0:T(8,128)(2,1)S(1)} %bitcast.56, bf16[64,512]{1,0:T(8,128)(2,1)S(1)} %bitcast.62), kind=kOutput, calls=%fused_computation.4 | convolution fusion | flops 477102080 | bytes 8323072 | tf_op jit(solution)/shard_map/rk,rc->kc/dot_general | solution.py:86
  165.7 16.0 %all-reduce.5.cloned.1.call-done = bf16[64,1024]{1,0:T(8,128)(2,1)} async-done(((bf16[64,1024]{1,0:T(8,128)(2,1)}), bf16[64,1024]{1,0:T(8,128)(2,1)}) %all-reduce.5.cloned.1.call-update) | async-done | bytes 131088 | tf_op jit(solution)/shard_map/psum | solution.py:35
  184.1 69.7 %reduce-scatter.13.cloned.1.call-done = bf16[128,1024]{1,0:T(8,128)(2,1)} async-done(((bf16[1024,1024]{1,0:T(8,128)(2,1)}), bf16[128,1024]{1,0:T(8,128)(2,1)}) %reduce-scatter.13.cloned.1.call-update) | async-done | bytes 262160
  255.8 68.8 %reduce-scatter.9.cloned.1.call-done = bf16[128,1024]{1,0:T(8,128)(2,1)} async-done(((bf16[1024,1024]{1,0:T(8,128)(2,1)}), bf16[128,1024]{1,0:T(8,128)(2,1)}) %reduce-scatter.9.cloned.1.call-update) | async-done | bytes 262160 | tf_op jit(solution)/shard_map/reduce_scatter | solution.py:130
  326.4 133.6 %reduce-scatter.11.cloned.1.call-done = bf16[896,512]{1,0:T(8,128)(2,1)} async-done(((bf16[7168,512]{1,0:T(8,128)(2,1)}), bf16[896,512]{1,0:T(8,128)(2,1)}) %reduce-scatter.11.cloned.1.call-update) | async-done | bytes 917520 | tf_op jit(solution)/shard_map/reduce_scatter | solution.py:84
  (79 shorter events, 38.3 us)
Async XLA Ops:
  7.2 9.2 %copy-start = (bf16[1024,1024]{1,0:T(8,128)(2,1)S(1)}, bf16[1024,1024]{1,0:T(8,128)(2,1)}, u32[]{:S(2)}) copy-start(bf16[1024,1024]{1,0:T(8,128)(2,1)} %param.13) | copy-start | bytes 6291460
  7.2 43.9 %all-reduce.3.cloned.1.call-start = ((), (), s32[]{:S(2)}) async-start(), calls=%async_computation.6 | async-start | bytes 262144 | tf_op jit(solution)/shard_map/psum | solution.py:35
  14.2 3.3 copy-start.5
  16.4 1.4 copy-start.3
  52.1 5.0 %collective-permute-start = (bf16[16,1024]{1,0:T(8,128)(2,1)S(1)}, bf16[16,1024]{1,0:T(8,128)(2,1)S(1)}, u32[]{:S(2)}, u32[]{:S(2)}) collective-permute-start(bf16[16,1024]{1,0:T(8,128)(2,1)S(1)} %get-tuple-element.33), channel_id=1, source_target_pairs={{0,4},{4,8},{8,12},{12,16},{16,20},{20,24},{24,28},{1,5},{5,9},{9,... | collective-permute-start | bytes 98312 | tf_op jit(solution)/shard_map/ppermute | solution.py:19
  55.4 5.8 %collective-permute-start.1 = (bf16[16,1024]{1,0:T(8,128)(2,1)S(1)}, bf16[16,1024]{1,0:T(8,128)(2,1)S(1)}, u32[]{:S(2)}, u32[]{:S(2)}) collective-permute-start(bf16[16,1024]{1,0:T(8,128)(2,1)S(1)} %get-tuple-element.34), channel_id=1, source_target_pairs={{4,0},{8,4},{12,8},{16,12},{20,16},{24,20},{28,24},{5,1},{9,5},{13... | collective-permute-start | bytes 98312 | tf_op jit(solution)/shard_map/ppermute | solution.py:20
  68.3 8.4 %copy-start.6 = (s32[64]{0:T(128)S(1)}, s32[64]{0:T(128)}, u32[]{:S(2)}) copy-start(s32[64]{0:T(128)} %param.16) | copy-start | bytes 772
  73.4 7.4 %all-to-all-start = ((bf16[4,16,512]{2,1,0:T(8,128)(2,1)}), bf16[4,16,512]{2,1,0:T(8,128)(2,1)S(1)}, u32[]{:S(2)}, u32[]{:S(2)}) async-start(bf16[4,16,512]{2,1,0:T(8,128)(2,1)} %bitcast), calls=%async_computation | async-start | bytes 131072 | tf_op jit(solution)/shard_map/all_to_all | solution.py:43
  86.6 7.4 %all-to-all-start.1 = ((bf16[4,16,512]{2,1,0:T(8,128)(2,1)}), bf16[4,16,512]{2,1,0:T(8,128)(2,1)S(1)}, u32[]{:S(2)}, u32[]{:S(2)}) async-start(bf16[4,16,512]{2,1,0:T(8,128)(2,1)} %copy.33), calls=%async_computation.1 | async-start | bytes 131072 | tf_op jit(solution)/shard_map/all_to_all | solution.py:43
  89.9 50.8 %reduce-scatter.7.cloned.1.call-start = ((), (), s32[]{:S(2)}) async-start(), calls=%async_computation.7 | async-start | bytes 163840 | tf_op jit(solution)/shard_map/reduce_scatter | solution.py:107
  110.1 6.6 %collective-permute-start.2 = (bf16[16,1024]{1,0:T(8,128)(2,1)S(1)}, bf16[16,1024]{1,0:T(8,128)(2,1)S(1)}, u32[]{:S(2)}, u32[]{:S(2)}) collective-permute-start(bf16[16,1024]{1,0:T(8,128)(2,1)S(1)} %get-tuple-element.29), channel_id=1, source_target_pairs={{0,4},{4,8},{8,12},{12,16},{16,20},{20,24},{24,28},{1,5},{5,9},{9,... | collective-permute-start | bytes 98312 | tf_op jit(solution)/shard_map/ppermute | solution.py:19
  114.4 5.8 %collective-permute-start.3 = (bf16[16,1024]{1,0:T(8,128)(2,1)S(1)}, bf16[16,1024]{1,0:T(8,128)(2,1)S(1)}, u32[]{:S(2)}, u32[]{:S(2)}) collective-permute-start(bf16[16,1024]{1,0:T(8,128)(2,1)S(1)} %get-tuple-element.30), channel_id=1, source_target_pairs={{4,0},{8,4},{12,8},{16,12},{20,16},{24,20},{28,24},{5,1},{9,5},{13... | collective-permute-start | bytes 98312 | tf_op jit(solution)/shard_map/ppermute | solution.py:20
  121.8 59.9 %all-reduce.5.cloned.1.call-start = ((), (), s32[]{:S(2)}) async-start(), calls=%async_computation.8 | async-start | bytes 262144 | tf_op jit(solution)/shard_map/psum | solution.py:35
  140.7 7.6 %copy-start.1 = (bf16[1024,1024]{1,0:T(8,128)(2,1)S(1)}, bf16[1024,1024]{1,0:T(8,128)(2,1)}, u32[]{:S(2)}) copy-start(bf16[1024,1024]{1,0:T(8,128)(2,1)} %param.12) | copy-start | bytes 6291460
  149.8 104.0 %reduce-scatter.13.cloned.1.call-start = ((), (), s32[]{:S(2)}) async-start(), calls=%async_computation.11 | async-start | bytes 2359296
  156.9 167.7 %reduce-scatter.9.cloned.1.call-start = ((), (), s32[]{:S(2)}) async-start(), calls=%async_computation.9 | async-start | bytes 2359296 | tf_op jit(solution)/shard_map/reduce_scatter | solution.py:130
  159.1 300.9 %reduce-scatter.11.cloned.1.call-start = ((), (), s32[]{:S(2)}) async-start(), calls=%async_computation.10 | async-start | bytes 8257536 | tf_op jit(solution)/shard_map/reduce_scatter | solution.py:84
  164.2 17.5 %copy-start.2 = (bf16[16,1024]{1,0:T(8,128)(2,1)S(1)}, bf16[16,1024]{1,0:T(8,128)(2,1)}, u32[]{:S(2)}) copy-start(bf16[16,1024]{1,0:T(8,128)(2,1)} %param.11) | copy-start | bytes 98308
  164.2 18.4 %copy-start.4 = (bf16[16,1024]{1,0:T(8,128)(2,1)S(1)}, bf16[16,1024]{1,0:T(8,128)(2,1)}, u32[]{:S(2)}) copy-start(bf16[16,1024]{1,0:T(8,128)(2,1)} %reduce-scatter.7.cloned.1.call-done) | copy-start | bytes 98308
Sparse Core Ops, SparseCore 0:
  17.7 33.3 all-reduce.2
  121.9 18.7 reduce-scatter.6
  149.9 31.7 all-reduce.4
  185.1 68.6 reduce-scatter.12
  257.2 67.3 reduce-scatter.8
  328.0 131.9 reduce-scatter.10
where the time goes:
time: 471 us; the launch traced here: 470 us
  waiting for transfers between devices  355 us (75%)
  matrix products  28.4 us (6%)
  local copies, waits for them, and re-layouts  22.6 us (5%)
  other arithmetic  19.4 us (4%)
  starting transfers between devices  17.1 us (4%)
  between operations  14.4 us (3%)
  blocking collectives  12.8 us (3%)
    reduce_scatter x1, waiting for transfers between devices, local(): lax.psum_scatter((jnp.einsum('rk,rc->kc', tap_rows, coarse_grad, preferre...  134 us
    unnamed x7, waiting for transfers between devices  69.8 us
    reduce_scatter x1, waiting for transfers between devices, local(): lax.psum_scatter((jnp.einsum('rd,rf->df', normed, pre_grad, preferred_ele...  68.8 us
    psum x2, waiting for transfers between devices, tp_sums(): return lax.psum(terms.astype(jnp.bfloat16), 'tp').astype(jnp.float32)  49.2 us
    reduce_scatter x1, waiting for transfers between devices, local(): lax.psum_scatter(partial_value.astype(jnp.bfloat16), 'tp', scatter_dimens...  18.8 us
    all_gather x2, blocking collectives, tp_rows(): return lax.all_gather(pieces, 'tp', axis=0, tiled=True)  12.8 us
  transfers between devices with their start and end apart: 12, of which 11 were waited for; matrix products, arithmetic and copies ran while one was open for 5% of the time, Pallas kernels for 0%

commit v1 on v0

--- a/solution.py
+++ b/solution.py
@@ -32,7 +32,7 @@
 
 
 def tp_sums(terms):
-    return lax.psum(terms.astype(jnp.bfloat16), "tp").astype(jnp.float32)
+    return jnp.sum(jax.lax.all_gather(terms.astype(jnp.bfloat16), "tp"), axis=0).astype(jnp.float32)
 
 
 def tile_margin(tile_data):

time: 471 us -> 412 us (0.87)
  waiting for transfers between devices: 355 us -> 282 us
  blocking collectives: 12.8 us -> 27.5 us
    psum x2 -> x0, waiting for transfers between devices: 49.2 us -> none  [tp_sums(): return lax.psum(terms.astype(jnp.bfloat16), 'tp').astype(jnp.float32)]
    unnamed x7 -> x5, waiting for transfers between devices: 69.8 us -> 46.4 us
    all_gather x0 -> x2, blocking collectives: none -> 14.8 us  [tp_sums(): jax.lax.all_gather(terms.astype(jnp.bfloat16), 'tp')]
  transfers between devices with their start and end apart: 12 -> 10, of which waited for: 11 -> 8; matrix products, arithmetic and copies ran while one was open for 5% -> 5% of each run, Pallas kernels for 0% -> 0%
where the time goes in v1:
time: 412 us; the launch traced here: 411 us
  waiting for transfers between devices  282 us (68%)
  matrix products  27.6 us (7%)
  blocking collectives  27.5 us (7%)
  local copies, waits for them, and re-layouts  24.8 us (6%)
  other arithmetic  17.2 us (4%)
  starting transfers between devices  17.1 us (4%)
  between operations  14.1 us (3%)
    reduce_scatter x1, waiting for transfers between devices, local(): lax.psum_scatter((jnp.einsum('rk,rc->kc', tap_rows, coarse_grad, preferre...  134 us
    reduce_scatter x1, waiting for transfers between devices, local(): lax.psum_scatter((jnp.einsum('rd,rf->df', normed, pre_grad, preferred_ele...  68.9 us
    unnamed x5, waiting for transfers between devices  46.4 us
    reduce_scatter x1, waiting for transfers between devices, local(): lax.psum_scatter(partial_value.astype(jnp.bfloat16), 'tp', scatter_dimens...  19 us
    all_gather x2, blocking collectives, tp_sums(): jax.lax.all_gather(terms.astype(jnp.bfloat16), 'tp')  14.8 us
    all_gather x2, blocking collectives, tp_rows(): return lax.all_gather(pieces, 'tp', axis=0, tiled=True)  12.7 us
  transfers between devices with their start and end apart: 10, of which 8 were waited for; matrix products, arithmetic and copies ran while one was open for 5% of the time, Pallas kernels for 0%

profile of v1, /device:TPU:0, one launch (start us, length us, event | category | flops | bytes accessed | tf_op | source)
XLA Modules:
  0.0 410.5 jit_solution(14272995744859670024)
XLA Ops:
  7.2 6.9 %all_gather.18 = bf16[64,1024]{1,0:T(8,128)(2,1)S(1)} all-gather(bf16[16,1024]{1,0:T(8,128)(2,1)} %param.11), channel_id=1, replica_groups=mesh['tile'=8,'tp'=4] {'tp'}, dimensions={0}, use_global_device_ids=true | all-gather | bytes 163840 | tf_op jit(solution)/shard_map/all_gather | solution.py:31
  17.5 7.6 %all-gather = bf16[256,1024]{1,0:T(8,128)(2,1)S(1)} all-gather(bf16[64,1024]{1,0:T(8,128)(2,1)S(1)} %convolution_convert_fusion.1), channel_id=2, replica_groups=mesh['tile'=8,'tp'=4] {'tp'}, dimensions={0}, use_global_device_ids=true | all-gather | bytes 655360 | tf_op jit(solution)/shard_map/all_gather | solution.py:35
  25.2 3.5 collective-permute-start
  30.5 4.0 collective-permute-done.1
  34.6 2.7 gather_fusion
  41.6 5.1 %convolution_convert_fusion.2 = bf16[64,512]{1,0:T(8,128)(2,1)} fusion(bf16[64,7168]{1,0:T(8,128)(2,1)S(1)} %bitcast.57, bf16[7168,512]{1,0:T(8,128)(2,1)} %param.14), kind=kOutput, calls=%fused_computation.11 | convolution fusion | flops 469794816 | bytes 8323072 | tf_op jit(solution)/shard_map/dot_general | solution.py:70
  46.7 3.3 all-to-all-start
  51.4 2.7 all-to-all-done
  59.8 3.3 all-to-all-start.1
  63.1 4.0 all-to-all-done.1
  67.2 6.6 %fusion.29 = f32[64,7168]{1,0:T(8,128)} fusion(bf16[64,512]{1,0:T(8,128)(2,1)S(1)} %bitcast.65, bf16[7168,512]{1,0:T(8,128)(2,1)} %param.14), kind=kOutput, calls=%fused_computation.66 | convolution fusion | flops 469762048 | bytes 9240576 | tf_op jit(solution)/shard_map/dot_general | solution.py:93
  73.8 2.7 reshape.194
  76.5 5.9 %scatter_custom_fusion.1 = f32[97,1024]{1,0:T(8,128)} fusion(s32[448]{0:T(512)S(1)} %bitcast.69, f32[448,1024]{1,0:T(8,128)} %reshape.194, f32[]{:T(128)} %constant.112.clone.1), kind=kCustom, calls=%fused_computation.22 | custom fusion | flops 458752 | bytes 397824 | tf_op jit(solution)/shard_map/scatter-add | solution.py:98
  83.4 4.4 %collective-permute-start.2 = (bf16[16,1024]{1,0:T(8,128)(2,1)S(1)}, bf16[16,1024]{1,0:T(8,128)(2,1)S(1)}, u32[]{:S(2)}, u32[]{:S(2)}) collective-permute-start(bf16[16,1024]{1,0:T(8,128)(2,1)S(1)} %get-tuple-element.29), channel_id=1, source_target_pairs={{0,4},{4,8},{8,12},{12,16},{16,20},{20,24},{24,28},{1,5},{5,9},{9,... | collective-permute-start | bytes 98312 | tf_op jit(solution)/shard_map/ppermute | solution.py:19
  90.1 3.5 collective-permute-done.3
  95.2 19.0 %reduce-scatter.7.cloned.1.call-done = bf16[16,1024]{1,0:T(8,128)(2,1)} async-done(((bf16[64,1024]{1,0:T(8,128)(2,1)}), bf16[16,1024]{1,0:T(8,128)(2,1)}) %reduce-scatter.7.cloned.1.call-update) | async-done | bytes 32784 | tf_op jit(solution)/shard_map/reduce_scatter | solution.py:107
  114.2 5.8 %all_gather.21 = bf16[64,1024]{1,0:T(8,128)(2,1)S(1)} all-gather(bf16[16,1024]{1,0:T(8,128)(2,1)} %reduce-scatter.7.cloned.1.call-done), channel_id=1, replica_groups=mesh['tile'=8,'tp'=4] {'tp'}, dimensions={0}, use_global_device_ids=true | all-gather | bytes 163840 | tf_op jit(solution)/shard_map/all_gather | solution.py:31
  122.8 4.0 copy.34
  131.6 5.1 %multiply_convert_fusion = bf16[7168,512]{1,0:T(8,128)(2,1)} fusion(bf16[64,7168]{1,0:T(8,128)(2,1)S(1)} %bitcast.58, bf16[64,512]{1,0:T(8,128)(2,1)S(1)} %bitcast.66), kind=kOutput, calls=%fused_computation.4 | convolution fusion | flops 477102080 | bytes 8323072 | tf_op jit(solution)/shard_map/rk,rc->kc/dot_general | solution.py:86
  140.5 7.3 %all-gather.1 = bf16[256,1024]{1,0:T(8,128)(2,1)S(1)} all-gather(bf16[64,1024]{1,0:T(8,128)(2,1)S(1)} %convolution_convert_fusion), channel_id=3, replica_groups=mesh['tile'=8,'tp'=4] {'tp'}, dimensions={0}, use_global_device_ids=true | all-gather | bytes 655360 | tf_op jit(solution)/shard_map/all_gather | solution.py:35
  148.8 46.3 %reduce-scatter.13.cloned.1.call-done = bf16[128,1024]{1,0:T(8,128)(2,1)} async-done(((bf16[1024,1024]{1,0:T(8,128)(2,1)}), bf16[128,1024]{1,0:T(8,128)(2,1)}) %reduce-scatter.13.cloned.1.call-update) | async-done | bytes 262160
  197.0 68.9 %reduce-scatter.9.cloned.1.call-done = bf16[128,1024]{1,0:T(8,128)(2,1)} async-done(((bf16[1024,1024]{1,0:T(8,128)(2,1)}), bf16[128,1024]{1,0:T(8,128)(2,1)}) %reduce-scatter.9.cloned.1.call-update) | async-done | bytes 262160 | tf_op jit(solution)/shard_map/reduce_scatter | solution.py:130
  267.8 133.6 %reduce-scatter.11.cloned.1.call-done = bf16[896,512]{1,0:T(8,128)(2,1)} async-done(((bf16[7168,512]{1,0:T(8,128)(2,1)}), bf16[896,512]{1,0:T(8,128)(2,1)}) %reduce-scatter.11.cloned.1.call-update) | async-done | bytes 917520 | tf_op jit(solution)/shard_map/reduce_scatter | solution.py:84
  401.3 2.7 convert_element_type.114
  (81 shorter events, 37.7 us)
Async XLA Ops:
  7.2 9.9 %copy-start = (bf16[1024,1024]{1,0:T(8,128)(2,1)S(1)}, bf16[1024,1024]{1,0:T(8,128)(2,1)}, u32[]{:S(2)}) copy-start(bf16[1024,1024]{1,0:T(8,128)(2,1)} %param.13) | copy-start | bytes 6291460
  16.3 0.7 copy-start.2
  17.0 13.0 %copy-start.7 = (s32[64,7]{0,1:T(8,128)S(1)}, s32[64,7]{0,1:T(8,128)}, u32[]{:S(2)}) copy-start(s32[64,7]{0,1:T(8,128)} %param.15) | copy-start | bytes 5380
  25.2 5.3 %collective-permute-start = (bf16[16,1024]{1,0:T(8,128)(2,1)S(1)}, bf16[16,1024]{1,0:T(8,128)(2,1)S(1)}, u32[]{:S(2)}, u32[]{:S(2)}) collective-permute-start(bf16[16,1024]{1,0:T(8,128)(2,1)S(1)} %get-tuple-element.33), channel_id=1, source_target_pairs={{0,4},{4,8},{8,12},{12,16},{16,20},{20,24},{24,28},{1,5},{5,9},{9,... | collective-permute-start | bytes 98312 | tf_op jit(solution)/shard_map/ppermute | solution.py:19
  28.7 5.8 %collective-permute-start.1 = (bf16[16,1024]{1,0:T(8,128)(2,1)S(1)}, bf16[16,1024]{1,0:T(8,128)(2,1)S(1)}, u32[]{:S(2)}, u32[]{:S(2)}) collective-permute-start(bf16[16,1024]{1,0:T(8,128)(2,1)S(1)} %get-tuple-element.34), channel_id=1, source_target_pairs={{4,0},{8,4},{12,8},{16,12},{20,16},{24,20},{28,24},{5,1},{9,5},{13... | collective-permute-start | bytes 98312 | tf_op jit(solution)/shard_map/ppermute | solution.py:20
  41.5 8.4 %copy-start.8 = (s32[64]{0:T(128)S(1)}, s32[64]{0:T(128)}, u32[]{:S(2)}) copy-start(s32[64]{0:T(128)} %param.16) | copy-start | bytes 772
  46.7 7.4 %all-to-all-start = ((bf16[4,16,512]{2,1,0:T(8,128)(2,1)}), bf16[4,16,512]{2,1,0:T(8,128)(2,1)S(1)}, u32[]{:S(2)}, u32[]{:S(2)}) async-start(bf16[4,16,512]{2,1,0:T(8,128)(2,1)} %bitcast.1), calls=%async_computation | async-start | bytes 131072 | tf_op jit(solution)/shard_map/all_to_all | solution.py:43
  59.8 7.4 %all-to-all-start.1 = ((bf16[4,16,512]{2,1,0:T(8,128)(2,1)}), bf16[4,16,512]{2,1,0:T(8,128)(2,1)S(1)}, u32[]{:S(2)}, u32[]{:S(2)}) async-start(bf16[4,16,512]{2,1,0:T(8,128)(2,1)} %copy.33), calls=%async_computation.1 | async-start | bytes 131072 | tf_op jit(solution)/shard_map/all_to_all | solution.py:43
  63.1 51.1 %reduce-scatter.7.cloned.1.call-start = ((), (), s32[]{:S(2)}) async-start(), calls=%async_computation.6 | async-start | bytes 163840 | tf_op jit(solution)/shard_map/reduce_scatter | solution.py:107
  76.5 44.2 %copy-start.3 = (f32[64,1024]{1,0:T(8,128)S(1)}, f32[64,1024]{1,0:T(8,128)}, u32[]{:S(2)}) copy-start(f32[64,1024]{1,0:T(8,128)} %copy-done.2) | copy-start | bytes 786436
  83.4 6.6 %collective-permute-start.2 = (bf16[16,1024]{1,0:T(8,128)(2,1)S(1)}, bf16[16,1024]{1,0:T(8,128)(2,1)S(1)}, u32[]{:S(2)}, u32[]{:S(2)}) collective-permute-start(bf16[16,1024]{1,0:T(8,128)(2,1)S(1)} %get-tuple-element.29), channel_id=1, source_target_pairs={{0,4},{4,8},{8,12},{12,16},{16,20},{20,24},{24,28},{1,5},{5,9},{9,... | collective-permute-start | bytes 98312 | tf_op jit(solution)/shard_map/ppermute | solution.py:19
  87.8 5.8 %collective-permute-start.3 = (bf16[16,1024]{1,0:T(8,128)(2,1)S(1)}, bf16[16,1024]{1,0:T(8,128)(2,1)S(1)}, u32[]{:S(2)}, u32[]{:S(2)}) collective-permute-start(bf16[16,1024]{1,0:T(8,128)(2,1)S(1)} %get-tuple-element.30), channel_id=1, source_target_pairs={{4,0},{8,4},{12,8},{16,12},{20,16},{24,20},{28,24},{5,1},{9,5},{13... | collective-permute-start | bytes 98312 | tf_op jit(solution)/shard_map/ppermute | solution.py:20
  95.2 99.9 %reduce-scatter.13.cloned.1.call-start = ((), (), s32[]{:S(2)}) async-start(), calls=%async_computation.9 | async-start | bytes 2359296
  120.0 0.7 copy-start.5
  126.8 0.9 copy-start.6
  126.8 139.2 %reduce-scatter.9.cloned.1.call-start = ((), (), s32[]{:S(2)}) async-start(), calls=%async_computation.7 | async-start | bytes 2359296 | tf_op jit(solution)/shard_map/reduce_scatter | solution.py:130
  131.5 269.8 %reduce-scatter.11.cloned.1.call-start = ((), (), s32[]{:S(2)}) async-start(), calls=%async_computation.8 | async-start | bytes 8257536 | tf_op jit(solution)/shard_map/reduce_scatter | solution.py:84
  136.7 11.2 %copy-start.1 = (bf16[16,1024]{1,0:T(8,128)(2,1)S(1)}, bf16[16,1024]{1,0:T(8,128)(2,1)}, u32[]{:S(2)}) copy-start(bf16[16,1024]{1,0:T(8,128)(2,1)} %param.11) | copy-start | bytes 98308
  136.8 11.3 %copy-start.4 = (bf16[16,1024]{1,0:T(8,128)(2,1)S(1)}, bf16[16,1024]{1,0:T(8,128)(2,1)}, u32[]{:S(2)}) copy-start(bf16[16,1024]{1,0:T(8,128)(2,1)} %reduce-scatter.7.cloned.1.call-done) | copy-start | bytes 98308
Sparse Core Ops, SparseCore 0:
  95.3 18.9 reduce-scatter.6
  126.9 68.1 reduce-scatter.12
  198.6 67.3 reduce-scatter.8
  269.4 131.8 reduce-scatter.10
